TPU v7x, 32 devices: a whole 2x2x4 slice. The times are simulated.
32 devices in a mesh: tm: 4 (over y, core), head: 2 (over x), branch: 4 (over z).
Axes of the slice: x: 2, y: 2, z: 4, core: 2. Of those that a mesh axis runs over, the one named last changes fastest.
Arguments:
- queries: bfloat16 [4, 4, 512, 20, 128], P('branch', 'tm', 'head'), may hold values from -8 to 8
- keys: bfloat16 [4, 4, 512, 20, 128], P('branch', 'tm', 'head'), may hold values from -5 to 5
- values: bfloat16 [4, 4, 512, 20, 128], P('branch', 'tm', 'head'), may hold values from -6 to 6
- ctx_keys: bfloat16 [4, 512, 20, 128], P('tm', ('head', 'branch')), may hold values from -5 to 5
- ctx_values: bfloat16 [4, 512, 20, 128], P('tm', ('head', 'branch')), may hold values from -6 to 6
- hidden: bfloat16 [4, 4, 512, 5120], P('branch', 'tm', 'head'), may hold values from -6 to 6
- out_weight: bfloat16 [2560, 5120], P('head'), may hold values from -0.5 to 0.5
- gates: float32 [16, 5120], replicated, may hold values from 0.5 to 2
- levels: int32 [4], replicated, may hold values from 0 to 15
- span_mask: int32 [4, 4], replicated, may hold values from 0 to 1, as said below
- prefix: int32 [1], replicated, may hold values from 1 to 3
Outputs:
- updated: bfloat16 [4, 4, 512, 5120], P('branch', 'tm', 'head')
Inputs may be any that keep to these rules, and one draw needn't show every extreme that they name: `span_mask`: 1 on the diagonal and in the first column, 0 above the diagonal.
All inputs are finite; a program needn't handle non-finite values.
Results may differ from a plain program's by a relative error of at most 0.01.
Values may be sent and summed in bfloat16 or wider, within the bound.
No kernel may reach another device: no remote copies, remote signals or barrier semaphores. Data moves between devices by JAX's collectives and lax.ppermute only.
A program may use at most 256 MiB of HBM per device.

v0:
```python
import math
import jax
import jax.numpy as jnp
from jax import lax
from jax.sharding import PartitionSpec as P

NEG_BIG = -1e30


def fold_block(running, key_block, heads_q, mask_row, score_scale):
    run_max, run_total, run_acc = running
    block_keys = key_block[0]
    block_values = key_block[1]
    row_count = block_keys.shape[0]
    span_len = heads_q.shape[0]
    row_span = jnp.arange(row_count, dtype=jnp.int32) // span_len
    span_hits = row_span[:, None] == jnp.arange(mask_row.shape[0], dtype=jnp.int32)[None, :]
    visible = jnp.sum(jnp.where(span_hits, mask_row[None, :], 0), axis=1) > 0
    scores = (
        jnp.einsum("qhd,khd->hqk", heads_q, block_keys, preferred_element_type=jnp.float32)
        * score_scale
    )
    block_max = jnp.max(jnp.where(visible[None, None, :], scores, NEG_BIG), axis=2)
    new_max = jnp.maximum(run_max, block_max)
    weights = jnp.where(visible[None, None, :], jnp.exp(scores - new_max[:, :, None]), 0.0)
    new_total = jnp.sum(weights, axis=2)
    new_acc = jnp.einsum(
        "hqk,khd->hqd",
        weights.astype(jnp.bfloat16),
        block_values,
        preferred_element_type=jnp.float32,
    )
    return (new_max, new_total, new_acc)


def body(
    queries,
    keys,
    values,
    ctx_keys,
    ctx_values,
    hidden,
    out_weight,
    gates,
    levels,
    span_mask,
    prefix,
):
    span_index = lax.axis_index("tm")
    heads_q, heads_k, heads_v = (
        lax.all_to_all(queries[0, 0], "head", split_axis=1, concat_axis=0, tiled=True),
        lax.all_to_all(keys[0, 0], "head", split_axis=1, concat_axis=0, tiled=True),
        lax.all_to_all(values[0, 0], "head", split_axis=1, concat_axis=0, tiled=True),
    )
    split_parts = (
        lax.all_to_all(ctx_keys[0], "head", split_axis=1, concat_axis=0, tiled=True),
        lax.all_to_all(ctx_values[0], "head", split_axis=1, concat_axis=0, tiled=True),
    )
    ctx_full_k, ctx_full_v = (
        lax.all_gather(split_parts[0], "branch", axis=0, tiled=True),
        lax.all_gather(split_parts[1], "branch", axis=0, tiled=True),
    )
    use_context = span_index < prefix[0]
    slot_kv = jnp.where(
        use_context, jnp.stack([ctx_full_k, ctx_full_v]), jnp.stack([heads_k, heads_v])
    )
    span_len = heads_q.shape[0]
    group_heads = heads_q.shape[1]
    head_dim = heads_q.shape[2]
    score_scale = 1.0 / math.sqrt(head_dim)
    mask_row = lax.dynamic_index_in_dim(span_mask, span_index, 0, keepdims=False)
    initial = (
        jnp.full((group_heads, span_len), NEG_BIG, jnp.float32),
        jnp.zeros((group_heads, span_len), jnp.float32),
        jnp.zeros((group_heads, span_len, head_dim), jnp.float32),
    )
    run_max, run_total, run_acc = fold_block(
        initial, lax.all_gather(slot_kv, "tm", axis=1, tiled=True), heads_q, mask_row, score_scale
    )
    attended = (run_acc / run_total[:, :, None]).astype(jnp.bfloat16)
    weight_heads = out_weight.reshape(group_heads, head_dim, out_weight.shape[1])
    projected = lax.psum_scatter(
        jnp.einsum(
            "hqd,hdn->qn", attended, weight_heads, preferred_element_type=jnp.float32
        ).astype(jnp.bfloat16),
        "head",
        scatter_dimension=0,
        tiled=True,
    ).astype(jnp.float32)
    level_now = lax.dynamic_index_in_dim(levels, span_index, 0, keepdims=False)
    gate_row = lax.dynamic_index_in_dim(gates, level_now, 0, keepdims=False)
    mixed_rows = hidden[0, 0].astype(jnp.float32) + gate_row[None, :] * projected
    return mixed_rows.astype(jnp.bfloat16)[None, None]


def solution(mesh):
    return jax.shard_map(
        body,
        mesh=mesh,
        in_specs=(
            P("branch", "tm", "head", None, None),
            P("branch", "tm", "head", None, None),
            P("branch", "tm", "head", None, None),
            P("tm", ("head", "branch"), None, None),
            P("tm", ("head", "branch"), None, None),
            P("branch", "tm", "head", None),
            P("head", None),
            P(),
            P(),
            P(),
            P(),
        ),
        out_specs=P("branch", "tm", "head", None),
        check_vma=False,
    )
```

profile of v0, /device:TPU:0, one launch (start us, length us, event | category | flops | bytes accessed | tf_op | source)
XLA Modules:
  0.0 301.1 jit_solution(17909818051579816194)
XLA Ops:
  6.5 0.0 copy-start
  6.5 0.0 all-gather.6.cloned.1.call-start
  6.5 10.9 %all_to_all.84 = bf16[64,20,128]{2,0,1:T(8,128)(2,1)S(1)} all-to-all(bf16[64,20,128]{2,0,1:T(8,128)(2,1)} %bitcast.86), channel_id=1, replica_groups=mesh['tm'=4,'head'=2,'branch'=4] {'head'}, dimensions={1} | all-to-all | bytes 655360 | tf_op jit(solution)/shard_map/all_to_all | solution.py:57
  17.5 0.7 copy.18
  18.2 0.0 all-gather.6.cloned.1.call-update
  18.3 0.0 all-gather.4.cloned.1.call-start
  18.3 9.0 %all_to_all.85 = bf16[64,20,128]{2,0,1:T(8,128)(2,1)S(1)} all-to-all(bf16[64,20,128]{2,0,1:T(8,128)(2,1)} %bitcast.87), channel_id=1, replica_groups=mesh['tm'=4,'head'=2,'branch'=4] {'head'}, dimensions={1} | all-to-all | bytes 655360 | tf_op jit(solution)/shard_map/all_to_all | solution.py:56
  27.3 0.7 copy.17
  28.1 0.0 all-gather.4.cloned.1.call-update
  28.1 18.9 %all_to_all.86 = bf16[256,20,128]{2,0,1:T(8,128)(2,1)S(1)} all-to-all(bf16[256,20,128]{2,0,1:T(8,128)(2,1)} %bitcast.77), channel_id=1, replica_groups=mesh['tm'=4,'head'=2,'branch'=4] {'head'}, dimensions={1} | all-to-all | bytes 2621440 | tf_op jit(solution)/shard_map/all_to_all | solution.py:52
  47.0 3.6 %all-to-all-start.3 = ((bf16[256,20,128]{2,0,1:T(8,128)(2,1)}), bf16[256,20,128]{2,0,1:T(8,128)(2,1)S(1)}, u32[]{:S(2)}, u32[]{:S(2)}) async-start(bf16[256,20,128]{2,0,1:T(8,128)(2,1)} %bitcast.78), calls=%async_computation.3 | async-start | bytes 2621440 | tf_op jit(solution)/shard_map/all_to_all | solution.py:53
  50.6 0.0 all-gather.8.cloned.1.call-start
  51.3 1.2 copy.19
  52.5 12.6 %all-to-all-done.3 = bf16[256,20,128]{2,0,1:T(8,128)(2,1)S(1)} async-done(((bf16[256,20,128]{2,0,1:T(8,128)(2,1)}), bf16[256,20,128]{2,0,1:T(8,128)(2,1)S(1)}, u32[]{:S(2)}, u32[]{:S(2)}) %all-to-all-start.3) | async-done | bytes 1310752 | tf_op jit(solution)/shard_map/all_to_all | solution.py:53
  65.1 0.1 copy.20
  65.2 0.0 all-gather.6.cloned.1.call-done
  65.2 19.5 %all-gather.4.cloned.1.call-done = bf16[512,10,128]{2,0,1:T(8,128)(2,1)} async-done(((bf16[128,10,128]{2,0,1:T(8,128)(2,1)}), bf16[512,10,128]{2,0,1:T(8,128)(2,1)}) %all-gather.4.cloned.1.call-update) | async-done | bytes 1310736 | tf_op jit(solution)/shard_map/all_gather | solution.py:60
  84.7 3.4 %maximum_select_fusion = bf16[2,512,10,128]{3,1,2,0:T(8,128)(2,1)} fusion(bf16[1,512,10,128]{3,1,2,0:T(8,128)(2,1)} %bitcast.84, bf16[1,512,10,128]{3,1,2,0:T(8,128)(2,1)} %bitcast.85, bf16[1,512,10,128]{3,1,2,0:T(8,128)(2,1)S(1)} %bitcast.76, bf16[1,512,10,128]{3,1,2,0:T(8,128)(2,1)} %bitcast.75, pred[]{:T(512)S(6)} %lt.15), kind=kLoop, calls=%fused_computation.13 | loop fusion | flops 3932160 | bytes 7864321 | tf_op jit(solution)/shard_map/jit(_where)/select_n | solution.py:64
  88.1 0.0 all-gather.8.cloned.1.call-update
  88.1 3.6 %all-to-all-start.4 = ((bf16[256,20,128]{2,0,1:T(8,128)(2,1)}), bf16[256,20,128]{2,0,1:T(8,128)(2,1)S(1)}, u32[]{:S(2)}, u32[]{:S(2)}) async-start(bf16[256,20,128]{2,0,1:T(8,128)(2,1)} %bitcast.24), calls=%async_computation.4 | async-start | bytes 2621440 | tf_op jit(solution)/shard_map/all_to_all | solution.py:51
  91.8 0.0 reduce-scatter.2.cloned.1.call-start
  91.8 0.7 dynamic-slice_bitcast_fusion
  92.5 0.1 select_reduce_fusion.1
  92.6 15.1 %all-to-all-done.4 = bf16[256,20,128]{2,0,1:T(8,128)(2,1)S(1)} async-done(((bf16[256,20,128]{2,0,1:T(8,128)(2,1)}), bf16[256,20,128]{2,0,1:T(8,128)(2,1)S(1)}, u32[]{:S(2)}, u32[]{:S(2)}) %all-to-all-start.4) | async-done | bytes 1310752 | tf_op jit(solution)/shard_map/all_to_all | solution.py:51
  107.7 0.1 copy.21
  107.8 49.7 %all-gather.8.cloned.1.call-done = bf16[2,2048,10,128]{3,1,2,0:T(8,128)(2,1)} async-done(((bf16[2,512,10,128]{3,1,2,0:T(8,128)(2,1)}), bf16[2,2048,10,128]{3,1,2,0:T(8,128)(2,1)}) %all-gather.8.cloned.1.call-update) | async-done | bytes 10485776 | tf_op jit(solution)/shard_map/all_gather | solution.py:78
  157.5 18.1 %select_reduce_fusion = (f32[10,512]{1,0:T(8,128)S(1)}, f32[10,2048,512]{2,1,0:T(8,128)}) fusion(pred[2048]{0:T(1024)(128)(4,1)S(1)} %broadcast_compare_fusion, bf16[512,10,128]{2,0,1:T(8,128)(2,1)S(1)} %bitcast.79, bf16[2,2048,10,128]{3,1,2,0:T(8,128)(2,1)} %all-gather.8.cloned.1.call-done), kind=kOutput, calls=%fused_computation.3 | convolution fusion | flops 2715806720 | bytes 48519168 | tf_op jit(solution)/shard_map/qhd,khd->hqk/dot_general | solution.py:20
  175.6 17.4 %bitcast_reduce_fusion = f32[10,512]{1,0:T(8,128)S(1)} fusion(f32[10,2048,512]{2,1,0:T(8,128)} %get-tuple-element.6, f32[10,512]{1,0:T(8,128)S(1)} %broadcast_maximum_fusion, pred[2048]{0:T(1024)(128)(4,1)S(1)} %broadcast_compare_fusion), kind=kLoop, calls=%fused_computation | loop fusion | flops 41937920 | bytes 41986048 | tf_op jit(solution)/shard_map/reduce_sum | solution.py:26
  193.1 19.8 %divide_convert_fusion.4 = bf16[10,512,128]{2,1,0:T(8,128)(2,1)S(1)} fusion(bf16[2,2048,10,128]{3,1,2,0:T(8,128)(2,1)} %all-gather.8.cloned.1.call-done, f32[10,2048,512]{2,1,0:T(8,128)} %get-tuple-element.6, f32[10,512]{1,0:T(8,128)S(1)} %broadcast_maximum_fusion, pred[2048]{0:T(1024)(128)(4,1)S(1)} %broadcast_compare_fusion, ...), kind=kOutput, calls=%fused_computation.14.clone.clone.1 | convolution fusion | flops 2727608320 | bytes 48539648 | tf_op jit(solution)/shard_map/hqk,khd->hqd/dot_general | solution.py:27
  212.9 11.5 %bitcast_convert_fusion.2 = bf16[512,5120]{1,0:T(8,128)(2,1)} fusion(bf16[10,128,5120]{2,1,0:T(8,128)(2,1)} %bitcast.89, bf16[10,512,128]{2,1,0:T(8,128)(2,1)S(1)} %divide_convert_fusion.4), kind=kOutput, calls=%fused_computation.6 | convolution fusion | flops 6713507840 | bytes 19660800 | tf_op jit(solution)/shard_map/hqd,hdn->qn/dot_general | solution.py:83
  224.4 0.0 copy-start.2
  224.4 0.0 copy-start.1
  224.4 0.0 reduce-scatter.2.cloned.1.call-update
  224.4 0.6 copy-done.2
  225.1 0.6 dynamic_slice.12
  227.6 0.0 copy-done
  227.6 62.7 %reduce-scatter.2.cloned.1.call-done = bf16[256,5120]{1,0:T(8,128)(2,1)} async-done(((bf16[512,5120]{1,0:T(8,128)(2,1)}), bf16[256,5120]{1,0:T(8,128)(2,1)}) %reduce-scatter.2.cloned.1.call-update) | async-done | bytes 2621456 | tf_op jit(solution)/shard_map/reduce_scatter | solution.py:82
  290.4 0.0 copy-done.1
  290.4 4.2 %fusion.4 = bf16[1,1,256,5120]{3,2,1,0:T(8,128)(2,1)} fusion(bf16[256,5120]{1,0:T(8,128)(2,1)} %reduce-scatter.2.cloned.1.call-done, bf16[1,1,256,5120]{3,2,1,0:T(8,128)(2,1)S(1)} %copy-done.1, f32[5120]{0:T(1024)S(1)} %bitcast.88), kind=kLoop, calls=%fused_computation.12 | loop fusion | flops 6553600 | bytes 7884800 | tf_op jit(solution)/shard_map/broadcast_in_dim | solution.py:93
  (4 shorter events, 0.0 us)
Async XLA Ops:
  6.5 221.1 %copy-start = (f32[16,5120]{1,0:T(8,128)S(1)}, f32[16,5120]{1,0:T(8,128)}, u32[]{:S(2)}) copy-start(f32[16,5120]{1,0:T(8,128)} %param.18) | copy-start | bytes 983044
  6.5 58.7 %all-gather.6.cloned.1.call-start = ((), (), s32[]{:S(2)}) async-start(), calls=%async_computation.7 | async-start | bytes 1638400 | tf_op jit(solution)/shard_map/all_gather | solution.py:61
  18.3 66.5 %all-gather.4.cloned.1.call-start = ((), (), s32[]{:S(2)}) async-start(), calls=%async_computation.6 | async-start | bytes 1638400 | tf_op jit(solution)/shard_map/all_gather | solution.py:60
  47.0 18.1 %all-to-all-start.3 = ((bf16[256,20,128]{2,0,1:T(8,128)(2,1)}), bf16[256,20,128]{2,0,1:T(8,128)(2,1)S(1)}, u32[]{:S(2)}, u32[]{:S(2)}) async-start(bf16[256,20,128]{2,0,1:T(8,128)(2,1)} %bitcast.78), calls=%async_computation.3 | async-start | bytes 2621440 | tf_op jit(solution)/shard_map/all_to_all | solution.py:53
  50.6 106.9 %all-gather.8.cloned.1.call-start = ((), (), s32[]{:S(2)}) async-start(), calls=%async_computation.8 | async-start | bytes 13107200 | tf_op jit(solution)/shard_map/all_gather | solution.py:78
  88.1 19.6 %all-to-all-start.4 = ((bf16[256,20,128]{2,0,1:T(8,128)(2,1)}), bf16[256,20,128]{2,0,1:T(8,128)(2,1)S(1)}, u32[]{:S(2)}, u32[]{:S(2)}) async-start(bf16[256,20,128]{2,0,1:T(8,128)(2,1)} %bitcast.24), calls=%async_computation.4 | async-start | bytes 2621440 | tf_op jit(solution)/shard_map/all_to_all | solution.py:51
  91.8 198.6 %reduce-scatter.2.cloned.1.call-start = ((), (), s32[]{:S(2)}) async-start(), calls=%async_computation.9 | async-start | bytes 7864320 | tf_op jit(solution)/shard_map/reduce_scatter | solution.py:82
  224.4 0.7 copy-start.2
  224.4 66.0 %copy-start.1 = (bf16[1,1,256,5120]{3,2,1,0:T(8,128)(2,1)S(1)}, bf16[1,1,256,5120]{3,2,1,0:T(8,128)(2,1)}, u32[]{:S(2)}) copy-start(bf16[1,1,256,5120]{3,2,1,0:T(8,128)(2,1)} %param.16) | copy-start | bytes 7864324
Sparse Core Ops, SparseCore 0:
  18.4 33.1 all-gather.5
  53.1 31.5 all-gather.3
  88.2 69.2 all-gather.7
  224.6 65.7 reduce-scatter.1
where the time goes:
time: 302 us; the launch traced here: 301 us
  waiting for transfers between devices  160 us (53%)
  matrix products  49.4 us (16%)
  blocking collectives  38.8 us (13%)
  other arithmetic  25.1 us (8%)
  between operations  15.8 us (5%)
  starting transfers between devices  7.39 us (2%)
  local copies, waits for them, and re-layouts  4.8 us (2%)
    reduce_scatter x1, waiting for transfers between devices, body(): lax.psum_scatter(jnp.einsum('hqd,hdn->qn', attended, weight_heads, prefer...  62.7 us
    all_gather x1, waiting for transfers between devices, body(): lax.all_gather(slot_kv, 'tm', axis=1, tiled=True)  49.7 us
    dot_general x1, matrix products, fold_block(): jnp.einsum('hqk,khd->hqd', weights.astype(jnp.bfloat16), block_values, pr...  19.8 us
    all_gather x1, waiting for transfers between devices, body(): lax.all_gather(split_parts[0], 'branch', axis=0, tiled=True)  19.5 us
    all_to_all x1, blocking collectives, body(): lax.all_to_all(keys[0, 0], 'head', split_axis=1, concat_axis=0, tiled=True)  18.9 us
    dot_general x1, matrix products, fold_block(): jnp.einsum('qhd,khd->hqk', heads_q, block_keys, preferred_element_type=jn...  18.1 us
    reduce_sum x1, other arithmetic, fold_block(): new_total = jnp.sum(weights, axis=2)  17.4 us
    all_to_all x1, waiting for transfers between devices, body(): lax.all_to_all(queries[0, 0], 'head', split_axis=1, concat_axis=0, tiled=...  15.1 us
  transfers between devices with their start and end apart: 6, of which 5 were waited for; matrix products, arithmetic and copies ran while one was open for 1% of the time, Pallas kernels for 0%

commit v1 on v0

--- a/solution.py
+++ b/solution.py
@@ -5,6 +5,27 @@
 from jax.sharding import PartitionSpec as P
 
 NEG_BIG = -1e30
+
+
+def gather_around(x, axis, dim):
+    length, mine, span = (lax.axis_size(axis), lax.axis_index(axis), x.shape[dim])
+    right = [(i, (i + 1) % length) for i in range(length)]
+    behind = [(i, (i - 1) % length) for i in range(length)]
+    out = jnp.zeros((*x.shape[:dim], length * span, *x.shape[dim + 1 :]), x.dtype)
+    out = lax.dynamic_update_slice_in_dim(out, x, mine * span, axis=dim)
+    from_left = from_right = x
+    halfway = length // 2
+    for step in range(1, halfway + 1):
+        from_left = lax.ppermute(from_left, axis, right)
+        out = lax.dynamic_update_slice_in_dim(
+            out, from_left, (mine - step) % length * span, axis=dim
+        )
+        if step < length - halfway:
+            from_right = lax.ppermute(from_right, axis, behind)
+            out = lax.dynamic_update_slice_in_dim(
+                out, from_right, (mine + step) % length * span, axis=dim
+            )
+    return out
 
 
 def fold_block(running, key_block, heads_q, mask_row, score_scale):
@@ -57,7 +78,7 @@
         lax.all_to_all(ctx_values[0], "head", split_axis=1, concat_axis=0, tiled=True),
     )
     ctx_full_k, ctx_full_v = (
-        lax.all_gather(split_parts[0], "branch", axis=0, tiled=True),
+        gather_around(split_parts[0], "branch", 0),
         lax.all_gather(split_parts[1], "branch", axis=0, tiled=True),
     )
     use_context = span_index < prefix[0]

time: 302 us -> 291 us (0.964)
  blocking collectives: 38.8 us -> 20 us
  starting transfers between devices: 7.39 us -> 16.1 us
  waiting for transfers between devices: 160 us -> 153 us
  local copies, waits for them, and re-layouts: 4.8 us -> 11.5 us
    all_gather x1 -> x0, waiting for transfers between devices: 19.5 us -> none  [body(): lax.all_gather(split_parts[0], 'branch', axis=0, tiled=True)]
    all_to_all x1 -> x0, blocking collectives: 18.9 us -> none  [body(): lax.all_to_all(keys[0, 0], 'head', split_axis=1, concat_axis=0, tiled=True)]
    all_to_all x0 -> x1, waiting for transfers between devices: none -> 13.4 us  [body(): lax.all_to_all(keys[0, 0], 'head', split_axis=1, concat_axis=0, tiled=True)]
    all_to_all x1, waiting for transfers between devices: 12.6 us -> 0.01 us  [body(): lax.all_to_all(values[0, 0], 'head', split_axis=1, concat_axis=0, tiled=T...]
    ppermute x0 -> x3, waiting for transfers between devices: none -> 12.5 us  [the longest x1 6.64 us: gather_around(): from_right = lax.ppermute(from_right, axis, behind)]
    dynamic_update_slice x0 -> x4, local copies, waits for them, and re-layouts: none -> 5.14 us  [the longest x2 3.57 us: gather_around(): lax.dynamic_update_slice_in_dim(out, from_left, (mine - step) % length *...]
    ppermute x0 -> x3, starting transfers between devices: none -> 5.12 us  [the longest x1 3.29 us: gather_around(): from_right = lax.ppermute(from_right, axis, behind)]
    all_to_all x0 -> x1, starting transfers between devices: none -> 3.63 us  [body(): lax.all_to_all(keys[0, 0], 'head', split_axis=1, concat_axis=0, tiled=True)]
  transfers between devices with their start and end apart: 6 -> 9, of which waited for: 5 -> 6; matrix products, arithmetic and copies ran while one was open for 1% -> 4% of each run, Pallas kernels for 0% -> 0%
where the time goes in v1:
time: 291 us
  waiting for transfers between devices  153 us (53%)
  matrix products  49.4 us (17%)
  other arithmetic  25.1 us (9%)
  blocking collectives  20 us (7%)
  starting transfers between devices  16.1 us (6%)
  between operations  15.9 us (5%)
  local copies, waits for them, and re-layouts  11.5 us (4%)
    reduce_scatter x1, waiting for transfers between devices, body(): lax.psum_scatter(jnp.einsum('hqd,hdn->qn', attended, weight_heads, prefer...  62.7 us
    all_gather x1, waiting for transfers between devices, body(): lax.all_gather(slot_kv, 'tm', axis=1, tiled=True)  49 us
    dot_general x1, matrix products, fold_block(): jnp.einsum('hqk,khd->hqd', weights.astype(jnp.bfloat16), block_values, pr...  19.9 us
    dot_general x1, matrix products, fold_block(): jnp.einsum('qhd,khd->hqk', heads_q, block_keys, preferred_element_type=jn...  18.1 us
    reduce_sum x1, other arithmetic, fold_block(): new_total = jnp.sum(weights, axis=2)  17.4 us
    all_to_all x1, waiting for transfers between devices, body(): lax.all_to_all(queries[0, 0], 'head', split_axis=1, concat_axis=0, tiled=...  14.8 us
    all_to_all x1, waiting for transfers between devices, body(): lax.all_to_all(keys[0, 0], 'head', split_axis=1, concat_axis=0, tiled=True)  13.4 us
    dot_general x1, matrix products, body(): jnp.einsum('hqd,hdn->qn', attended, weight_heads, preferred_element_type=...  11.5 us
  transfers between devices with their start and end apart: 9, of which 6 were waited for; matrix products, arithmetic and copies ran while one was open for 4% of the time, Pallas kernels for 0%

profile of v1, /device:TPU:0, one launch (start us, length us, event | category | flops | bytes accessed | tf_op | source)
XLA Modules:
  0.0 290.5 jit_solution(10859154314464583453)
XLA Ops:
  6.5 0.0 copy-start
  6.5 0.0 all-gather.3.cloned.1.call-start
  6.5 10.9 %all_to_all.84 = bf16[64,20,128]{2,0,1:T(8,128)(2,1)S(1)} all-to-all(bf16[64,20,128]{2,0,1:T(8,128)(2,1)} %bitcast.94), channel_id=1, replica_groups=mesh['tm'=4,'head'=2,'branch'=4] {'head'}, dimensions={1} | all-to-all | bytes 655360 | tf_op jit(solution)/shard_map/all_to_all | solution.py:78
  17.5 0.7 copy.18
  18.2 0.0 all-gather.3.cloned.1.call-update
  18.2 9.0 %all_to_all.85 = bf16[64,20,128]{2,0,1:T(8,128)(2,1)S(1)} all-to-all(bf16[64,20,128]{2,0,1:T(8,128)(2,1)} %bitcast.95), channel_id=1, replica_groups=mesh['tm'=4,'head'=2,'branch'=4] {'head'}, dimensions={1} | all-to-all | bytes 655360 | tf_op jit(solution)/shard_map/all_to_all | solution.py:77
  27.3 3.6 %all-to-all-start.2 = ((bf16[256,20,128]{2,0,1:T(8,128)(2,1)}), bf16[256,20,128]{2,0,1:T(8,128)(2,1)S(1)}, u32[]{:S(2)}, u32[]{:S(2)}) async-start(bf16[256,20,128]{2,0,1:T(8,128)(2,1)} %bitcast.84), calls=%async_computation.2 | async-start | bytes 2621440 | tf_op jit(solution)/shard_map/all_to_all | solution.py:73
  30.9 1.8 collective-permute-start
  32.8 13.4 %all-to-all-done.2 = bf16[256,20,128]{2,0,1:T(8,128)(2,1)S(1)} async-done(((bf16[256,20,128]{2,0,1:T(8,128)(2,1)}), bf16[256,20,128]{2,0,1:T(8,128)(2,1)S(1)}, u32[]{:S(2)}, u32[]{:S(2)}) %all-to-all-start.2) | async-done | bytes 1310752 | tf_op jit(solution)/shard_map/all_to_all | solution.py:73
  46.1 3.6 %all-to-all-start.3 = ((bf16[256,20,128]{2,0,1:T(8,128)(2,1)}), bf16[256,20,128]{2,0,1:T(8,128)(2,1)S(1)}, u32[]{:S(2)}, u32[]{:S(2)}) async-start(bf16[256,20,128]{2,0,1:T(8,128)(2,1)} %bitcast.85), calls=%async_computation.3 | async-start | bytes 2621440 | tf_op jit(solution)/shard_map/all_to_all | solution.py:74
  49.8 0.0 all-gather.5.cloned.1.call-start
  50.5 3.3 %collective-permute-start.1 = (bf16[128,10,128]{2,0,1:T(8,128)(2,1)S(1)}, bf16[128,10,128]{2,0,1:T(8,128)(2,1)S(1)}, u32[]{:S(2)}, u32[]{:S(2)}) collective-permute-start(bf16[128,10,128]{2,0,1:T(8,128)(2,1)S(1)} %bitcast.89), channel_id=1, source_target_pairs={{0,3},{1,0},{2,1},{3,2},{4,7},{5,4},{6,5},{7,6},{8,11},{9,8},{10,9... | collective-permute-start | bytes 983048 | tf_op jit(solution)/shard_map/ppermute | solution.py:24
  53.8 1.3 stack.26
  55.1 0.8 constant_dynamic-update-slice_fusion
  55.9 0.0 collective-permute-done
  55.9 0.0 collective-permute-start.2
  55.9 1.8 bitcast_dynamic-update-slice_fusion.2
  57.7 6.6 %collective-permute-done.1 = bf16[128,10,128]{2,0,1:T(8,128)(2,1)S(1)} collective-permute-done((bf16[128,10,128]{2,0,1:T(8,128)(2,1)S(1)}, bf16[128,10,128]{2,0,1:T(8,128)(2,1)S(1)}, u32[]{:S(2)}, u32[]{:S(2)}) %collective-permute-start.1) | collective-permute-done | bytes 327712 | tf_op jit(solution)/shard_map/ppermute | solution.py:24
  64.3 0.8 bitcast_dynamic-update-slice_fusion.1
  65.1 1.1 copy.19
  66.2 0.0 copy-start.1
  66.2 0.0 all-to-all-done.3
  66.2 1.1 copy.20
  67.4 5.9 %collective-permute-done.2 = bf16[128,10,128]{2,0,1:T(8,128)(2,1)} collective-permute-done((bf16[128,10,128]{2,0,1:T(8,128)(2,1)}, bf16[128,10,128]{2,0,1:T(8,128)(2,1)}, u32[]{:S(2)}, u32[]{:S(2)}) %collective-permute-start.2) | collective-permute-done | bytes 327712 | tf_op jit(solution)/shard_map/ppermute | solution.py:19
  73.3 1.8 bitcast_dynamic-update-slice_fusion
  75.0 0.0 all-gather.3.cloned.1.call-done
  75.0 0.0 copy-done.1
  75.0 3.4 %maximum_select_fusion = bf16[2,512,10,128]{3,1,2,0:T(8,128)(2,1)} fusion(bf16[1,512,10,128]{3,1,2,0:T(8,128)(2,1)} %bitcast.93, bf16[1,512,10,128]{3,1,2,0:T(8,128)(2,1)} %bitcast_dynamic-update-slice_fusion, bf16[1,512,10,128]{3,1,2,0:T(8,128)(2,1)} %bitcast.83, bf16[1,512,10,128]{3,1,2,0:T(8,128)(2,1)S(1)} %bitcast.82, pred[]{:T(512)S(6)} %lt.41), kind=kLoop, calls=%fused_computation.13 | loop fusion | flops 3932160 | bytes 7864321 | tf_op jit(solution)/shard_map/jit(_where)/select_n | solution.py:85
  78.4 0.0 all-gather.5.cloned.1.call-update
  78.4 3.6 %all-to-all-start.4 = ((bf16[256,20,128]{2,0,1:T(8,128)(2,1)}), bf16[256,20,128]{2,0,1:T(8,128)(2,1)S(1)}, u32[]{:S(2)}, u32[]{:S(2)}) async-start(bf16[256,20,128]{2,0,1:T(8,128)(2,1)} %bitcast.28), calls=%async_computation.4 | async-start | bytes 2621440 | tf_op jit(solution)/shard_map/all_to_all | solution.py:72
  82.1 0.0 reduce-scatter.2.cloned.1.call-start
  82.1 0.7 fusion.9
  82.8 0.1 select_reduce_fusion.1
  82.9 14.8 %all-to-all-done.4 = bf16[256,20,128]{2,0,1:T(8,128)(2,1)S(1)} async-done(((bf16[256,20,128]{2,0,1:T(8,128)(2,1)}), bf16[256,20,128]{2,0,1:T(8,128)(2,1)S(1)}, u32[]{:S(2)}, u32[]{:S(2)}) %all-to-all-start.4) | async-done | bytes 1310752 | tf_op jit(solution)/shard_map/all_to_all | solution.py:72
  97.8 0.1 copy.21
  97.9 49.0 %all-gather.5.cloned.1.call-done = bf16[2,2048,10,128]{3,1,2,0:T(8,128)(2,1)} async-done(((bf16[2,512,10,128]{3,1,2,0:T(8,128)(2,1)}), bf16[2,2048,10,128]{3,1,2,0:T(8,128)(2,1)}) %all-gather.5.cloned.1.call-update) | async-done | bytes 10485776 | tf_op jit(solution)/shard_map/all_gather | solution.py:99
  146.9 18.1 %select_reduce_fusion = (f32[10,512]{1,0:T(8,128)S(1)}, f32[10,2048,512]{2,1,0:T(8,128)}) fusion(pred[2048]{0:T(1024)(128)(4,1)S(1)} %broadcast_compare_fusion, bf16[512,10,128]{2,0,1:T(8,128)(2,1)S(1)} %bitcast.86, bf16[2,2048,10,128]{3,1,2,0:T(8,128)(2,1)} %all-gather.5.cloned.1.call-done), kind=kOutput, calls=%fused_computation.3 | convolution fusion | flops 2715806720 | bytes 48519168 | tf_op jit(solution)/shard_map/qhd,khd->hqk/dot_general | solution.py:41
  165.0 17.4 %bitcast_reduce_fusion = f32[10,512]{1,0:T(8,128)S(1)} fusion(f32[10,2048,512]{2,1,0:T(8,128)} %get-tuple-element.6, f32[10,512]{1,0:T(8,128)S(1)} %broadcast_maximum_fusion, pred[2048]{0:T(1024)(128)(4,1)S(1)} %broadcast_compare_fusion), kind=kLoop, calls=%fused_computation | loop fusion | flops 41937920 | bytes 41986048 | tf_op jit(solution)/shard_map/reduce_sum | solution.py:47
  182.4 19.9 %divide_convert_fusion.4 = bf16[10,512,128]{2,1,0:T(8,128)(2,1)S(1)} fusion(bf16[2,2048,10,128]{3,1,2,0:T(8,128)(2,1)} %all-gather.5.cloned.1.call-done, f32[10,2048,512]{2,1,0:T(8,128)} %get-tuple-element.6, f32[10,512]{1,0:T(8,128)S(1)} %broadcast_maximum_fusion, pred[2048]{0:T(1024)(128)(4,1)S(1)} %broadcast_compare_fusion, ...), kind=kOutput, calls=%fused_computation.14.clone.clone.1 | convolution fusion | flops 2727608320 | bytes 48539648 | tf_op jit(solution)/shard_map/hqk,khd->hqd/dot_general | solution.py:48
  202.3 11.5 %bitcast_convert_fusion.2 = bf16[512,5120]{1,0:T(8,128)(2,1)} fusion(bf16[10,128,5120]{2,1,0:T(8,128)(2,1)} %bitcast.97, bf16[10,512,128]{2,1,0:T(8,128)(2,1)S(1)} %divide_convert_fusion.4), kind=kOutput, calls=%fused_computation.6 | convolution fusion | flops 6713507840 | bytes 19660800 | tf_op jit(solution)/shard_map/hqd,hdn->qn/dot_general | solution.py:104
  213.8 0.0 copy-start.3
  213.8 0.0 copy-start.2
  213.8 0.0 reduce-scatter.2.cloned.1.call-update
  213.8 0.6 copy-done.3
  214.5 0.6 dynamic_slice.12
  217.0 0.0 copy-done
  217.0 62.7 %reduce-scatter.2.cloned.1.call-done = bf16[256,5120]{1,0:T(8,128)(2,1)} async-done(((bf16[512,5120]{1,0:T(8,128)(2,1)}), bf16[256,5120]{1,0:T(8,128)(2,1)}) %reduce-scatter.2.cloned.1.call-update) | async-done | bytes 2621456 | tf_op jit(solution)/shard_map/reduce_scatter | solution.py:103
  279.8 0.0 copy-done.2
  279.8 4.2 %fusion.4 = bf16[1,1,256,5120]{3,2,1,0:T(8,128)(2,1)} fusion(bf16[256,5120]{1,0:T(8,128)(2,1)} %reduce-scatter.2.cloned.1.call-done, bf16[1,1,256,5120]{3,2,1,0:T(8,128)(2,1)S(1)} %copy-done.2, f32[5120]{0:T(1024)S(1)} %bitcast.96), kind=kLoop, calls=%fused_computation.12 | loop fusion | flops 6553600 | bytes 7884800 | tf_op jit(solution)/shard_map/broadcast_in_dim | solution.py:114
  (5 shorter events, 0.1 us)
Async XLA Ops:
  6.5 210.5 %copy-start = (f32[16,5120]{1,0:T(8,128)S(1)}, f32[16,5120]{1,0:T(8,128)}, u32[]{:S(2)}) copy-start(f32[16,5120]{1,0:T(8,128)} %param.18) | copy-start | bytes 983044
  6.5 68.5 %all-gather.3.cloned.1.call-start = ((), (), s32[]{:S(2)}) async-start(), calls=%async_computation.6 | async-start | bytes 1638400 | tf_op jit(solution)/shard_map/all_gather | solution.py:82
  27.3 18.9 %all-to-all-start.2 = ((bf16[256,20,128]{2,0,1:T(8,128)(2,1)}), bf16[256,20,128]{2,0,1:T(8,128)(2,1)S(1)}, u32[]{:S(2)}, u32[]{:S(2)}) async-start(bf16[256,20,128]{2,0,1:T(8,128)(2,1)} %bitcast.84), calls=%async_computation.2 | async-start | bytes 2621440 | tf_op jit(solution)/shard_map/all_to_all | solution.py:73
  30.9 24.9 %collective-permute-start = (bf16[128,10,128]{2,0,1:T(8,128)(2,1)S(1)}, bf16[128,10,128]{2,0,1:T(8,128)(2,1)}, u32[]{:S(2)}, u32[]{:S(2)}) collective-permute-start(bf16[128,10,128]{2,0,1:T(8,128)(2,1)S(1)} %bitcast.88), channel_id=1, source_target_pairs={{0,1},{1,2},{2,3},{3,0},{4,5},{5,6},{6,7},{7,4},{8,9},{9,10},{10,1... | collective-permute-start | bytes 983048 | tf_op jit(solution)/shard_map/ppermute | solution.py:19
  46.1 20.1 %all-to-all-start.3 = ((bf16[256,20,128]{2,0,1:T(8,128)(2,1)}), bf16[256,20,128]{2,0,1:T(8,128)(2,1)S(1)}, u32[]{:S(2)}, u32[]{:S(2)}) async-start(bf16[256,20,128]{2,0,1:T(8,128)(2,1)} %bitcast.85), calls=%async_computation.3 | async-start | bytes 2621440 | tf_op jit(solution)/shard_map/all_to_all | solution.py:74
  49.8 97.1 %all-gather.5.cloned.1.call-start = ((), (), s32[]{:S(2)}) async-start(), calls=%async_computation.7 | async-start | bytes 13107200 | tf_op jit(solution)/shard_map/all_gather | solution.py:99
  50.5 13.8 %collective-permute-start.1 = (bf16[128,10,128]{2,0,1:T(8,128)(2,1)S(1)}, bf16[128,10,128]{2,0,1:T(8,128)(2,1)S(1)}, u32[]{:S(2)}, u32[]{:S(2)}) collective-permute-start(bf16[128,10,128]{2,0,1:T(8,128)(2,1)S(1)} %bitcast.89), channel_id=1, source_target_pairs={{0,3},{1,0},{2,1},{3,2},{4,7},{5,4},{6,5},{7,6},{8,11},{9,8},{10,9... | collective-permute-start | bytes 983048 | tf_op jit(solution)/shard_map/ppermute | solution.py:24
  55.9 17.4 %collective-permute-start.2 = (bf16[128,10,128]{2,0,1:T(8,128)(2,1)}, bf16[128,10,128]{2,0,1:T(8,128)(2,1)}, u32[]{:S(2)}, u32[]{:S(2)}) collective-permute-start(bf16[128,10,128]{2,0,1:T(8,128)(2,1)} %collective-permute-done), channel_id=1, source_target_pairs={{0,1},{1,2},{2,3},{3,0},{4,5},{5,6},{6,7},{7,4},{8,9},{9,10},{10,1... | collective-permute-start | bytes 983048 | tf_op jit(solution)/shard_map/ppermute | solution.py:19
  66.2 8.8 %copy-start.1 = (bf16[256,2,10,128]{3,0,1,2:T(8,128)(2,1)S(1)}, bf16[256,2,10,128]{3,0,1,2:T(8,128)(2,1)}, u32[]{:S(2)}) copy-start(bf16[256,2,10,128]{3,0,1,2:T(8,128)(2,1)} %copy.19) | copy-start | bytes 3932164
  78.4 19.3 %all-to-all-start.4 = ((bf16[256,20,128]{2,0,1:T(8,128)(2,1)}), bf16[256,20,128]{2,0,1:T(8,128)(2,1)S(1)}, u32[]{:S(2)}, u32[]{:S(2)}) async-start(bf16[256,20,128]{2,0,1:T(8,128)(2,1)} %bitcast.28), calls=%async_computation.4 | async-start | bytes 2621440 | tf_op jit(solution)/shard_map/all_to_all | solution.py:72
  82.1 197.7 %reduce-scatter.2.cloned.1.call-start = ((), (), s32[]{:S(2)}) async-start(), calls=%async_computation.8 | async-start | bytes 7864320 | tf_op jit(solution)/shard_map/reduce_scatter | solution.py:103
  213.8 0.7 copy-start.3
  213.8 66.0 %copy-start.2 = (bf16[1,1,256,5120]{3,2,1,0:T(8,128)(2,1)S(1)}, bf16[1,1,256,5120]{3,2,1,0:T(8,128)(2,1)}, u32[]{:S(2)}) copy-start(bf16[1,1,256,5120]{3,2,1,0:T(8,128)(2,1)} %param.16) | copy-start | bytes 7864324
Sparse Core Ops, SparseCore 0:
  18.4 42.4 all-gather.2
  78.6 68.3 all-gather.4
  214.0 65.7 reduce-scatter.1
